TPU v7x, 128 devices: a whole 4x4x4 slice. The times are simulated.
128 devices in a mesh: mb: 4 (over y), feat: 32 (over z, x, core).
Axes of the slice: x: 4, y: 4, z: 4, core: 2. Of those that a mesh axis runs over, the one named last changes fastest.
Arguments:
- features: float32 [1024, 262144], P('feat', 'mb'), may hold values from -6 to 6
- tile_rows: int32 [768], P('mb'), may hold values from 0 to 127
- tile_cols: int32 [768], P('mb'), may hold values from 0 to 511
- tile_masks: int32 [768, 128, 128], P('mb'), may hold values 0 or 1
- weight: bfloat16 [1024, 256], replicated, may hold values from -0.5625 to 0.5625
- upstream: bfloat16 [65536, 256], P(('mb', 'feat')), may hold values from -6 to 6
Outputs:
- activation: bfloat16 [65536, 256], P(('mb', 'feat'))
- weight_grad: float32 [1024, 256], P('feat')
All inputs are finite; a program needn't handle non-finite values. No bound on the sum of `tile_masks` on one device may be relied on, other than what follows from the above.
Results may differ from a plain program's by a relative error of at most 0.0063.
Values may be sent and summed in bfloat16 or wider, within the bound.
No kernel may reach another device: no remote copies, remote signals or barrier semaphores. Data moves between devices by JAX's collectives and lax.ppermute only.
A program may use at most 128 MiB of HBM per device.

v0:
```python
import jax
import jax.numpy as jnp
from jax import lax
from jax.sharding import PartitionSpec as P

NT = 16384


def smooth_gate(values):
    return 0.5 * values * (1.0 + lax.erf(values * 0.7071067811865476))


def gate_slope(values):
    return (
        0.5 * (1.0 + lax.erf(values * 0.7071067811865476))
        + values * jnp.exp(-0.5 * values * values) * 0.3989422804014327
    )


def neighbor_mean(sources, row_index, col_index, masks):
    feat_cols = sources.shape[0]
    src_count = sources.shape[1]
    tile_size = masks.shape[1]
    row_tiles = NT // tile_size
    blocks = sources.reshape(feat_cols, src_count // tile_size, tile_size)
    picked = jnp.take(blocks, col_index, axis=1)
    weights = masks.astype(jnp.float32)
    contrib = jnp.einsum("fts,tds->tfd", picked, weights, precision=lax.Precision.HIGHEST)
    onehot = (row_index[None, :] == jnp.arange(row_tiles, dtype=jnp.int32)[:, None]).astype(
        jnp.float32
    )
    summed = jnp.einsum("rt,tfd->frd", onehot, contrib, precision=lax.Precision.HIGHEST).reshape(
        feat_cols, NT
    )
    degree = jnp.dot(onehot, jnp.sum(weights, axis=2), precision=lax.Precision.HIGHEST).reshape(NT)
    return ((sources[:, :NT] + summed) / (degree[None, :] + 1.0)).astype(jnp.bfloat16)


def per_device(features, tile_rows, tile_cols, tile_masks, weight, upstream):
    hidden_t = neighbor_mean(features, tile_rows, tile_cols, tile_masks)
    feat_cols = hidden_t.shape[0]
    weight_part = lax.dynamic_slice_in_dim(weight, lax.axis_index("feat") * feat_cols, feat_cols, 0)
    picked = hidden_t
    preact = lax.psum_scatter(
        lax.dot_general(
            picked, weight_part, (((0,), (0,)), ((), ())), preferred_element_type=jnp.float32
        ),
        "feat",
        scatter_dimension=0,
        tiled=True,
    )
    slopes = (upstream.astype(jnp.float32) * gate_slope(preact)).astype(jnp.bfloat16)
    picked = hidden_t
    local_grad = jnp.dot(
        picked,
        lax.all_gather(slopes, "feat", axis=0, tiled=True),
        preferred_element_type=jnp.float32,
    )
    activation = smooth_gate(preact).astype(jnp.bfloat16)
    weight_grad = lax.psum(local_grad, "mb")
    return (activation, weight_grad)


def solution(mesh):
    return jax.shard_map(
        per_device,
        mesh=mesh,
        in_specs=(
            P("feat", "mb"),
            P("mb"),
            P("mb"),
            P("mb", None, None),
            P(),
            P(("mb", "feat"), None),
        ),
        out_specs=(P(("mb", "feat"), None), P("feat", None)),
        check_vma=False,
    )
```

profile of v0, /device:TPU:0, one launch (start us, length us, event | category | flops | bytes accessed | tf_op | source)
XLA Modules:
  0.0 273.4 jit_solution(18257796936870843259)
XLA Ops:
  7.2 0.0 copy-start
  7.2 0.0 reduce-scatter.2.cloned.1.call-start
  7.2 0.7 compare_and_fusion
  8.0 0.7 compare_select_fusion
  8.7 7.9 %convert_reduce_fusion = f32[192,128]{1,0:T(8,128)S(1)} fusion(s32[192,128,128]{2,1,0:T(8,128)} %param.9), kind=kLoop, calls=%fused_computation.1 | loop fusion | flops 6266880 | bytes 12681216 | tf_op jit(solution)/shard_map/reduce_sum | solution.py:35
  16.5 0.0 copy-start.3
  16.6 7.8 %copy_bitcast_fusion = f32[32,512,128]{2,0,1:T(8,128)} fusion(f32[32,65536]{1,0:T(8,128)} %param.6), kind=kLoop, calls=%fused_computation.4 | loop fusion | bytes 16777216 | tf_op jit(solution)/shard_map/reshape | solution.py:25
  24.4 0.0 copy-done.3
  24.4 0.4 fusion.13
  24.8 5.9 %gather_fusion = f32[192,32,128]{2,1,0:T(8,128)} fusion(f32[32,512,128]{2,0,1:T(8,128)} %copy_bitcast_fusion, s32[1024]{0:T(1024)S(1)} %pad_clamp_fusion), kind=kCustom, calls=%fused_computation | custom fusion | bytes 6292224 | tf_op jit(solution)/shard_map/jit(_take)/gather | solution.py:26
  30.6 22.4 %fusion = f32[192,32,128]{2,1,0:T(8,128)S(1)} fusion(s32[192,128,128]{2,1,0:T(8,128)} %param.9, f32[192,32,128]{2,1,0:T(8,128)} %gather_fusion, pred[192]{0:T(512)(128)(4,1)S(1)} %compare_and_fusion), kind=kOutput, calls=%fused_computation.2 | convolution fusion | flops 1211891712 | bytes 18874560 | tf_op jit(solution)/shard_map/fts,tds->tfd/dot_general | solution.py:28
  53.1 4.7 %fusion.8 = f32[32,128,128]{1,2,0:T(8,128)S(1)} fusion(f32[192,32,128]{2,1,0:T(8,128)S(1)} %fusion, s32[192]{0:T(256)S(1)} %copy-done.3), kind=kOutput, calls=%fused_computation.12 | convolution fusion | flops 1207984128 | bytes 5243648 | tf_op jit(solution)/shard_map/rt,tfd->frd/dot_general | solution.py:32
  57.8 1.9 copy.11
  59.6 3.5 %fusion.7 = bf16[32,16384]{1,0:T(8,128)(2,1)S(1)} fusion(f32[4,8,128,128]{3,2,1,0:T(8,128)} %bitcast.26, f32[32,65536]{1,0:T(8,128)} %param.6, f32[16384]{0:T(1024)S(1)} %fusion.13), kind=kLoop, calls=%fused_computation.11 | loop fusion | flops 1572864 | bytes 5308416 | tf_op jit(solution)/shard_map/convert_element_type | solution.py:36
  63.1 0.0 copy-done
  63.1 8.1 %fusion.24 = f32[16384,256]{1,0:T(8,128)} fusion(bf16[32,16384]{1,0:T(8,128)(2,1)S(1)} %fusion.7, bf16[1024,256]{1,0:T(8,128)(2,1)S(1)} %copy-done, s32[]{:T(128)S(6)} %select_n.14), kind=kOutput, calls=%fused_computation.30 | convolution fusion | flops 268435456 | bytes 17842180 | tf_op jit(solution)/shard_map/dot_general | solution.py:45
  71.2 0.0 copy-start.2
  71.2 0.0 reduce-scatter.2.cloned.1.call-update
  71.3 0.0 all-gather.2.cloned.1.call-start
  71.3 118.2 %reduce-scatter.2.cloned.1.call-done = f32[512,256]{1,0:T(8,128)} async-done(((f32[16384,256]{1,0:T(8,128)}), f32[512,256]{1,0:T(8,128)}) %reduce-scatter.2.cloned.1.call-update) | async-done | bytes 524304 | tf_op jit(solution)/shard_map/reduce_scatter | solution.py:44
  189.5 0.0 copy-done.2
  189.5 2.1 fusion.19
  191.7 0.0 all-gather.2.cloned.1.call-update
  191.7 52.2 %all-gather.2.cloned.1.call-done = bf16[16384,256]{1,0:T(8,128)(2,1)} async-done(((bf16[512,256]{1,0:T(8,128)(2,1)}), bf16[16384,256]{1,0:T(8,128)(2,1)}) %all-gather.2.cloned.1.call-update) | async-done | bytes 8388624 | tf_op jit(solution)/shard_map/all_gather | solution.py:56
  243.9 0.0 copy-start.1
  243.9 5.0 %fusion.28 = f32[32,256]{1,0:T(8,128)S(1)} fusion(bf16[32,16384]{1,0:T(8,128)(2,1)S(1)} %fusion.7, bf16[16384,256]{1,0:T(8,128)(2,1)} %all-gather.2.cloned.1.call-done), kind=kOutput, calls=%fused_computation.37 | convolution fusion | flops 268435456 | bytes 9469952 | tf_op jit(solution)/shard_map/dot_general | solution.py:54
  248.9 17.6 %psum.7 = f32[32,256]{1,0:T(8,128)} all-reduce(f32[32,256]{1,0:T(8,128)S(1)} %fusion.28), channel_id=1, replica_groups=mesh['mb'=4,'feat'=32] {'mb'}, use_global_device_ids=true, to_apply=%region_2.3 | all-reduce | flops 8192 | bytes 65536 | tf_op jit(solution)/shard_map/psum | solution.py:60
  266.5 0.0 copy-done.1
  (1 shorter events, 0.0 us)
Async XLA Ops:
  7.2 55.9 %copy-start = (bf16[1024,256]{1,0:T(8,128)(2,1)S(1)}, bf16[1024,256]{1,0:T(8,128)(2,1)}, u32[]{:S(2)}) copy-start(bf16[1024,256]{1,0:T(8,128)(2,1)} %param.10) | copy-start | bytes 1572868
  7.2 182.4 %reduce-scatter.2.cloned.1.call-start = ((), (), s32[]{:S(2)}) async-start(), calls=%async_computation.1 | async-start | bytes 17301504 | tf_op jit(solution)/shard_map/reduce_scatter | solution.py:44
  16.5 7.8 %copy-start.3 = (s32[192]{0:T(256)S(1)}, s32[192]{0:T(256)}, u32[]{:S(2)}) copy-start(s32[192]{0:T(256)} %param.7) | copy-start | bytes 2308
  71.2 118.3 %copy-start.2 = (bf16[512,256]{1,0:T(8,128)(2,1)S(1)}, bf16[512,256]{1,0:T(8,128)(2,1)}, u32[]{:S(2)}) copy-start(bf16[512,256]{1,0:T(8,128)(2,1)} %param.11) | copy-start | bytes 786436
  71.3 172.7 %all-gather.2.cloned.1.call-start = ((), (), s32[]{:S(2)}) async-start(), calls=%async_computation.2 | async-start | bytes 8650752 | tf_op jit(solution)/shard_map/all_gather | solution.py:56
  243.9 22.6 %copy-start.1 = (bf16[1024,256]{1,0:T(8,128)(2,1)S(1)}, bf16[1024,256]{1,0:T(8,128)(2,1)}, u32[]{:S(2)}) copy-start(bf16[1024,256]{1,0:T(8,128)(2,1)} %param.10) | copy-start | bytes 1572868
Sparse Core Ops, SparseCore 0:
  71.4 118.1 reduce-scatter.1
  191.8 52.0 all-gather.1
where the time goes:
time: 274 us; the launch traced here: 273 us
  waiting for transfers between devices  170 us (62%)
  matrix products  40.6 us (15%)
  blocking collectives  17.6 us (6%)
  local copies, waits for them, and re-layouts  15.6 us (6%)
  other arithmetic  14.9 us (5%)
  between operations  14.1 us (5%)
    reduce_scatter x1, waiting for transfers between devices, per_device(): lax.psum_scatter(lax.dot_general(picked, weight_part, (((0,), (0,)), ((),...  118 us
    all_gather x1, waiting for transfers between devices, per_device(): lax.all_gather(slopes, 'feat', axis=0, tiled=True)  52.2 us
    dot_general x1, matrix products, neighbor_mean(): jnp.einsum('fts,tds->tfd', picked, weights, precision=lax.Precision.HIGHEST)  22.4 us
    psum x1, blocking collectives, per_device(): weight_grad = lax.psum(local_grad, 'mb')  17.6 us
    dot_general x1, matrix products, per_device(): lax.dot_general(picked, weight_part, (((0,), (0,)), ((), ())), preferred_...  8.13 us
    reduce_sum x1, other arithmetic, neighbor_mean(): jnp.sum(weights, axis=2)  7.89 us
    reshape x1, local copies, waits for them, and re-layouts, neighbor_mean(): blocks = sources.reshape(feat_cols, src_count // tile_size, tile_size)  7.81 us
    gather x1, local copies, waits for them, and re-layouts, neighbor_mean(): picked = jnp.take(blocks, col_index, axis=1)  5.89 us
  transfers between devices with their start and end apart: 2, of which 2 were waited for; matrix products, arithmetic and copies ran while one was open for 0% of the time, Pallas kernels for 0%

commit v1 on v0

--- a/solution.py
+++ b/solution.py
@@ -4,6 +4,11 @@
 from jax.sharding import PartitionSpec as P
 
 NT = 16384
+
+
+def tiled_gather(x, axis, dim):
+    copies = jnp.concatenate([x] * lax.axis_size(axis), axis=dim)
+    return lax.all_to_all(copies, axis, dim, dim, tiled=True)
 
 
 def smooth_gate(values):
@@ -52,9 +57,7 @@
     slopes = (upstream.astype(jnp.float32) * gate_slope(preact)).astype(jnp.bfloat16)
     picked = hidden_t
     local_grad = jnp.dot(
-        picked,
-        lax.all_gather(slopes, "feat", axis=0, tiled=True),
-        preferred_element_type=jnp.float32,
+        picked, tiled_gather(slopes, "feat", 0), preferred_element_type=jnp.float32
     )
     activation = smooth_gate(preact).astype(jnp.bfloat16)
     weight_grad = lax.psum(local_grad, "mb")

time: 274 us -> 336 us (1.23)
  waiting for transfers between devices: 170 us -> 223 us
  starting transfers between devices: 0.08 us -> 5.53 us
  local copies, waits for them, and re-layouts: 15.6 us -> 19.4 us
    all_to_all x0 -> x1, waiting for transfers between devices: none -> 105 us  [tiled_gather(): return lax.all_to_all(copies, axis, dim, dim, tiled=True)]
    all_gather x1 -> x0, waiting for transfers between devices: 52.2 us -> none  [per_device(): lax.all_gather(slopes, 'feat', axis=0, tiled=True)]
    all_to_all x0 -> x1, starting transfers between devices: none -> 5.49 us  [tiled_gather(): return lax.all_to_all(copies, axis, dim, dim, tiled=True)]
    unnamed x8 -> x42, local copies, waits for them, and re-layouts: 0.03 us -> 3.83 us
where the time goes in v1:
time: 336 us
  waiting for transfers between devices  223 us (66%)
  matrix products  40.6 us (12%)
  local copies, waits for them, and re-layouts  19.4 us (6%)
  blocking collectives  17.6 us (5%)
  other arithmetic  14.8 us (4%)
  between operations  14.4 us (4%)
  starting transfers between devices  5.53 us (2%)
    reduce_scatter x1, waiting for transfers between devices, per_device(): lax.psum_scatter(lax.dot_general(picked, weight_part, (((0,), (0,)), ((),...  118 us
    all_to_all x1, waiting for transfers between devices, tiled_gather(): return lax.all_to_all(copies, axis, dim, dim, tiled=True)  105 us
    dot_general x1, matrix products, neighbor_mean(): jnp.einsum('fts,tds->tfd', picked, weights, precision=lax.Precision.HIGHEST)  22.4 us
    psum x1, blocking collectives, per_device(): weight_grad = lax.psum(local_grad, 'mb')  17.6 us
    dot_general x1, matrix products, per_device(): lax.dot_general(picked, weight_part, (((0,), (0,)), ((), ())), preferred_...  8.12 us
    reduce_sum x1, other arithmetic, neighbor_mean(): jnp.sum(weights, axis=2)  7.89 us
    reshape x1, local copies, waits for them, and re-layouts, neighbor_mean(): blocks = sources.reshape(feat_cols, src_count // tile_size, tile_size)  7.81 us
  transfers between devices with their start and end apart: 2, of which 2 were waited for; matrix products, arithmetic and copies ran while one was open for 0% of the time, Pallas kernels for 0%

profile of v1, /device:TPU:0, one launch (start us, length us, event | category | flops | bytes accessed | tf_op | source)
XLA Modules:
  0.0 335.7 jit_solution(15606494299120997235)
XLA Ops:
  7.2 0.0 copy-start
  7.2 0.0 reduce-scatter.2.cloned.1.call-start
  7.2 0.7 compare_and_fusion
  8.0 0.7 compare_select_fusion
  8.7 7.9 %convert_reduce_fusion = f32[192,128]{1,0:T(8,128)S(1)} fusion(s32[192,128,128]{2,1,0:T(8,128)} %param.9), kind=kLoop, calls=%fused_computation.1 | loop fusion | flops 6266880 | bytes 12681216 | tf_op jit(solution)/shard_map/reduce_sum | solution.py:40
  16.5 0.0 copy-start.5
  16.6 7.8 %copy_bitcast_fusion = f32[32,512,128]{2,0,1:T(8,128)} fusion(f32[32,65536]{1,0:T(8,128)} %param.6), kind=kLoop, calls=%fused_computation.4 | loop fusion | bytes 16777216 | tf_op jit(solution)/shard_map/reshape | solution.py:30
  24.4 0.0 copy-done.5
  24.4 0.4 fusion.13
  24.7 5.9 %gather_fusion = f32[192,32,128]{2,1,0:T(8,128)} fusion(f32[32,512,128]{2,0,1:T(8,128)} %copy_bitcast_fusion, s32[1024]{0:T(1024)S(1)} %pad_clamp_fusion), kind=kCustom, calls=%fused_computation | custom fusion | bytes 6292224 | tf_op jit(solution)/shard_map/jit(_take)/gather | solution.py:31
  30.6 22.4 %fusion = f32[192,32,128]{2,1,0:T(8,128)S(1)} fusion(s32[192,128,128]{2,1,0:T(8,128)} %param.9, f32[192,32,128]{2,1,0:T(8,128)} %gather_fusion, pred[192]{0:T(512)(128)(4,1)S(1)} %compare_and_fusion), kind=kOutput, calls=%fused_computation.2 | convolution fusion | flops 1211891712 | bytes 18874560 | tf_op jit(solution)/shard_map/fts,tds->tfd/dot_general | solution.py:33
  53.1 4.7 %fusion.8 = f32[32,128,128]{1,2,0:T(8,128)S(1)} fusion(f32[192,32,128]{2,1,0:T(8,128)S(1)} %fusion, s32[192]{0:T(256)S(1)} %copy-done.5), kind=kOutput, calls=%fused_computation.12 | convolution fusion | flops 1207984128 | bytes 5243648 | tf_op jit(solution)/shard_map/rt,tfd->frd/dot_general | solution.py:37
  57.8 1.9 copy.11
  59.6 3.5 %fusion.7 = bf16[32,16384]{1,0:T(8,128)(2,1)S(1)} fusion(f32[4,8,128,128]{3,2,1,0:T(8,128)} %bitcast.29, f32[32,65536]{1,0:T(8,128)} %param.6, f32[16384]{0:T(1024)S(1)} %fusion.13), kind=kLoop, calls=%fused_computation.11 | loop fusion | flops 1572864 | bytes 5308416 | tf_op jit(solution)/shard_map/convert_element_type | solution.py:41
  63.1 0.0 copy-done
  63.1 8.1 %fusion.24 = f32[16384,256]{1,0:T(8,128)} fusion(bf16[32,16384]{1,0:T(8,128)(2,1)S(1)} %fusion.7, bf16[1024,256]{1,0:T(8,128)(2,1)S(1)} %copy-done, s32[]{:T(128)S(6)} %select_n.14), kind=kOutput, calls=%fused_computation.62 | convolution fusion | flops 268435456 | bytes 17842180 | tf_op jit(solution)/shard_map/dot_general | solution.py:50
  71.2 0.0 copy-start.4
  71.2 0.0 reduce-scatter.2.cloned.1.call-update
  71.2 118.3 %reduce-scatter.2.cloned.1.call-done = f32[512,256]{1,0:T(8,128)} async-done(((f32[16384,256]{1,0:T(8,128)}), f32[512,256]{1,0:T(8,128)}) %reduce-scatter.2.cloned.1.call-update) | async-done | bytes 524304 | tf_op jit(solution)/shard_map/reduce_scatter | solution.py:49
  189.5 0.0 copy-done.4
  189.5 1.3 constant_dynamic-update-slice_fusion.31
  191.6 0.0 copy-start.2
  191.7 3.2 copy-done.2
  194.9 0.0 copy-start.3
  194.9 5.5 %all-to-all-start = ((bf16[32,512,256]{2,1,0:T(8,128)(2,1)}), bf16[32,512,256]{2,1,0:T(8,128)(2,1)}, u32[]{:S(2)}, u32[]{:S(2)}) async-start(bf16[32,512,256]{2,1,0:T(8,128)(2,1)} %bitcast.28), calls=%async_computation.1 | async-start | bytes 16777216 | tf_op jit(solution)/shard_map/all_to_all | solution.py:11
  200.4 0.0 copy-done.3
  200.4 0.8 multiply_convert_fusion
  201.2 105.0 %all-to-all-done = bf16[32,512,256]{2,1,0:T(8,128)(2,1)} async-done(((bf16[32,512,256]{2,1,0:T(8,128)(2,1)}), bf16[32,512,256]{2,1,0:T(8,128)(2,1)}, u32[]{:S(2)}, u32[]{:S(2)}) %all-to-all-start) | async-done | bytes 8388640 | tf_op jit(solution)/shard_map/all_to_all | solution.py:11
  306.2 0.0 copy-start.1
  306.2 5.0 %fusion.29 = f32[32,256]{1,0:T(8,128)S(1)} fusion(bf16[32,16384]{1,0:T(8,128)(2,1)S(1)} %fusion.7, bf16[16384,256]{1,0:T(8,128)(2,1)} %bitcast.5), kind=kOutput, calls=%fused_computation.69 | convolution fusion | flops 268435456 | bytes 9469952 | tf_op jit(solution)/shard_map/dot_general | solution.py:59
  311.2 17.6 %psum.7 = f32[32,256]{1,0:T(8,128)} all-reduce(f32[32,256]{1,0:T(8,128)S(1)} %fusion.29), channel_id=1, replica_groups=mesh['mb'=4,'feat'=32] {'mb'}, use_global_device_ids=true, to_apply=%region_2.3 | all-reduce | flops 8192 | bytes 65536 | tf_op jit(solution)/shard_map/psum | solution.py:63
  328.8 0.0 copy-done.1
  (32 shorter events, 0.6 us)
Async XLA Ops:
  7.2 55.9 %copy-start = (bf16[1024,256]{1,0:T(8,128)(2,1)S(1)}, bf16[1024,256]{1,0:T(8,128)(2,1)}, u32[]{:S(2)}) copy-start(bf16[1024,256]{1,0:T(8,128)(2,1)} %param.10) | copy-start | bytes 1572868
  7.2 182.3 %reduce-scatter.2.cloned.1.call-start = ((), (), s32[]{:S(2)}) async-start(), calls=%async_computation.2 | async-start | bytes 17301504 | tf_op jit(solution)/shard_map/reduce_scatter | solution.py:49
  16.5 7.8 %copy-start.5 = (s32[192]{0:T(256)S(1)}, s32[192]{0:T(256)}, u32[]{:S(2)}) copy-start(s32[192]{0:T(256)} %param.7) | copy-start | bytes 2308
  71.2 118.3 %copy-start.4 = (bf16[512,256]{1,0:T(8,128)(2,1)S(1)}, bf16[512,256]{1,0:T(8,128)(2,1)}, u32[]{:S(2)}) copy-start(bf16[512,256]{1,0:T(8,128)(2,1)} %param.11) | copy-start | bytes 786436
  191.6 3.2 copy-start.2
  194.9 5.5 %copy-start.3 = (f32[512,256]{1,0:T(8,128)S(1)}, f32[512,256]{1,0:T(8,128)}, u32[]{:S(2)}) copy-start(f32[512,256]{1,0:T(8,128)} %reduce-scatter.2.cloned.1.call-done) | copy-start | bytes 1572868
  194.9 111.4 %all-to-all-start = ((bf16[32,512,256]{2,1,0:T(8,128)(2,1)}), bf16[32,512,256]{2,1,0:T(8,128)(2,1)}, u32[]{:S(2)}, u32[]{:S(2)}) async-start(bf16[32,512,256]{2,1,0:T(8,128)(2,1)} %bitcast.28), calls=%async_computation.1 | async-start | bytes 16777216 | tf_op jit(solution)/shard_map/all_to_all | solution.py:11
  306.2 22.6 %copy-start.1 = (bf16[1024,256]{1,0:T(8,128)(2,1)S(1)}, bf16[1024,256]{1,0:T(8,128)(2,1)}, u32[]{:S(2)}) copy-start(bf16[1024,256]{1,0:T(8,128)(2,1)} %param.10) | copy-start | bytes 1572868
Sparse Core Ops, SparseCore 0:
  71.4 118.1 reduce-scatter.1
